TPU v7x, 32 devices: a whole 2x2x4 slice. The times are simulated.
32 devices in a mesh: dp: 8 (over z, x), tensor: 4 (over y, core).
Axes of the slice: x: 2, y: 2, z: 4, core: 2. Of those that a mesh axis runs over, the one named last changes fastest.
Arguments:
- inputs: bfloat16 [1500, 8, 1024], P('tensor', 'dp'), may hold values from -6 to 6
- segments: int32 [8, 1500], P('dp'), may hold values from 0 to 3, never falling along the last dimension, each value on 1 to 750 neighbouring positions
- cotangent: bfloat16 [1500, 8, 1024], P('tensor', 'dp'), may hold values from -6 to 6
- gain_one: float32 [1024], replicated, may hold values from 0.1 to 1.9
- first_in: bfloat16 [1024, 4096], P(None, 'tensor'), may hold values from -0.1875 to 0.1875
- first_out: bfloat16 [4096, 1024], P('tensor'), may hold values from -0.1875 to 0.1875
- gain_two: float32 [1024], replicated, may hold values from 0.1 to 1.9
- w_query: bfloat16 [1024, 1024], P(None, 'tensor'), may hold values from -0.1875 to 0.1875
- w_key: bfloat16 [1024, 1024], P(None, 'tensor'), may hold values from -0.1875 to 0.1875
- w_value: bfloat16 [1024, 1024], P(None, 'tensor'), may hold values from -0.1875 to 0.1875
- w_output: bfloat16 [1024, 1024], P('tensor'), may hold values from -0.75 to 0.75
- rel_table: float32 [16, 257], P('tensor'), may hold values from -4 to 4
- gain_three: float32 [1024], replicated, may hold values from 0.1 to 1.9
- w_glu: bfloat16 [1024, 2, 1024], P(None, None, 'tensor'), may hold values from -0.1875 to 0.1875
- kernel: float32 [31, 1024], P(None, 'tensor'), may hold values from -1 to 1
- w_back: bfloat16 [1024, 1024], P('tensor'), may hold values from -0.5 to 0.5
- gain_four: float32 [1024], replicated, may hold values from 0.1 to 1.9
- second_in: bfloat16 [1024, 4096], P(None, 'tensor'), may hold values from -0.1875 to 0.1875
- second_out: bfloat16 [4096, 1024], P('tensor'), may hold values from -0.1875 to 0.1875
- gain_five: float32 [1024], replicated, may hold values from 0.1 to 1.9
Outputs:
- output: bfloat16 [1500, 8, 1024], P('tensor', 'dp')
- grad_inputs: float32 [1500, 8, 1024], P('tensor', 'dp')
- grad_gain_one: float32 [1024], replicated
- grad_first_in: float32 [1024, 4096], P('dp', 'tensor')
- grad_first_out: float32 [4096, 1024], P('tensor', 'dp')
- grad_gain_two: float32 [1024], replicated
- grad_w_query: float32 [1024, 1024], P('dp', 'tensor')
- grad_w_key: float32 [1024, 1024], P('dp', 'tensor')
- grad_w_value: float32 [1024, 1024], P('dp', 'tensor')
- grad_w_output: float32 [1024, 1024], P('tensor', 'dp')
- grad_rel_table: float32 [16, 257], P('tensor')
- grad_gain_three: float32 [1024], replicated
- grad_w_glu: float32 [1024, 2, 1024], P('dp', None, 'tensor')
- grad_kernel: float32 [31, 1024], P(None, 'tensor')
- grad_w_back: float32 [1024, 1024], P('tensor', 'dp')
- grad_gain_four: float32 [1024], replicated
- grad_second_in: float32 [1024, 4096], P('dp', 'tensor')
- grad_second_out: float32 [4096, 1024], P('tensor', 'dp')
- grad_gain_five: float32 [1024], replicated
Inputs may be any that keep to these rules, and one draw needn't show every extreme that they name: `segments`: within each row of 1500 frames the segment numbers start at 0 and never fall; each of the 4 utterances holds 1 to 750 frames, and one holds exactly 750.
All inputs are finite; a program needn't handle non-finite values.
Results may differ from a plain program's by a relative error of at most 0.03.
Values may be sent and summed in bfloat16 or wider, within the bound.
No kernel may reach another device: no remote copies, remote signals or barrier semaphores. Data moves between devices by JAX's collectives and lax.ppermute only.
A program may use at most 256 MiB of HBM per device.

v0:
```python
import jax
import jax.numpy as jnp
from jax import lax
from jax.sharding import PartitionSpec as P

masked_score = -1e30


def normed(residual, gain_vec):
    row_mean = jnp.mean(residual, axis=-1, keepdims=True)
    centred = residual - row_mean
    variance = jnp.mean(centred * centred, axis=-1, keepdims=True)
    return centred * lax.rsqrt(variance + 1e-05) * gain_vec


def depthwise(values, kernel, labels):
    kernel_len = kernel.shape[0]
    half_width = kernel_len // 2
    frames = values.shape[0]
    padded = jnp.pad(values, ((half_width, half_width),) + ((0, 0),) * (values.ndim - 1))
    padded_labels = jnp.pad(
        labels, ((half_width, half_width),) + ((0, 0),) * (labels.ndim - 1), constant_values=-1
    )
    summed = jnp.zeros_like(values)
    for offset in range(kernel_len):
        same_seg = (padded_labels[offset : offset + frames] == labels)[..., None]
        summed = summed + jnp.where(
            same_seg, padded[offset : offset + frames] * kernel[offset], 0.0
        )
    return summed


def rel_band(table_row, frames):
    reach_max = table_row.shape[0] // 2
    distance = jnp.arange(2 * frames, dtype=jnp.int32) - (frames - 1)
    column = jnp.clip(distance, -reach_max, reach_max) + reach_max
    onehot = (column[None, :] == jnp.arange(table_row.shape[0], dtype=jnp.int32)[:, None]).astype(
        jnp.float32
    )
    diagonal_vals = jnp.dot(
        table_row, onehot, precision=lax.Precision.HIGHEST, preferred_element_type=jnp.float32
    )
    tiled = jnp.tile(diagonal_vals, frames)[: frames * (2 * frames - 1)]
    return tiled.reshape(frames, 2 * frames - 1)[:, frames - 1 :]


def gated_conv(glu_input, kernel, labels):
    channels = kernel.shape[1]
    gated = glu_input[..., :channels] * jax.nn.sigmoid(glu_input[..., channels:])
    return jax.nn.silu(depthwise(gated, kernel, labels))


def share_frames(local_rows):
    return lax.all_gather(local_rows, "tensor", axis=0, tiled=True)


def share_grads(local_rows):
    return lax.all_gather(local_rows, "tensor", axis=0, tiled=True)


def products(operands, transposed):
    summed = 0.0
    for operand, weight in operands:
        if transposed:
            summed = summed + jnp.einsum(
                "src,dc->srd", operand, weight, preferred_element_type=jnp.float32
            )
        else:
            summed = summed + jnp.einsum(
                "src,cd->srd", operand, weight, preferred_element_type=jnp.float32
            )
    return summed


def forward_sum(operands):
    return lax.psum_scatter(
        products(operands, False).astype(jnp.bfloat16), "tensor", scatter_dimension=0, tiled=True
    ).astype(jnp.float32)


def backward_sum(operands):
    return lax.psum_scatter(
        products(operands, True).astype(jnp.bfloat16), "tensor", scatter_dimension=0, tiled=True
    ).astype(jnp.float32)


def settle(grad_in, grad_out):
    return (
        lax.psum_scatter(grad_in, "dp", scatter_dimension=0, tiled=True),
        lax.psum_scatter(grad_out, "dp", scatter_dimension=1, tiled=True),
    )


def per_head(array, row_count, head_count):
    frames = array.shape[0]
    head_width = array.shape[2] // head_count
    return (
        array.reshape(frames, row_count, head_count, head_width)
        .transpose(1, 2, 0, 3)
        .reshape(row_count * head_count, frames, head_width)
    )


def per_frame(array, row_count, head_count):
    entries, frames, head_width = array.shape
    return (
        array.reshape(row_count, head_count, frames, head_width)
        .transpose(2, 0, 1, 3)
        .reshape(frames, row_count, head_count * head_width)
    )


def head_scores(query_head, key_head, rel_bias, label_row):
    score_scale = query_head.shape[-1] ** (-0.5)
    raw_scores = (
        jnp.einsum("qd,kd->qk", query_head, key_head, preferred_element_type=jnp.float32)
        * score_scale
        + rel_bias
    )
    allowed = label_row[:, None] == label_row[None, :]
    return jnp.where(allowed, raw_scores, masked_score)


def feed_forward(residual, gain_vec, w_in, w_out):
    local_rows = normed(residual, gain_vec).astype(jnp.bfloat16)
    gathered = share_frames(local_rows)
    hidden = jnp.einsum("srd,df->srf", gathered, w_in, preferred_element_type=jnp.float32)
    active = jax.nn.silu(hidden).astype(jnp.bfloat16)
    branch = forward_sum(((active, w_out),))
    return (residual + 0.5 * branch, (gathered, hidden, active))


def feed_back(incoming, residual, gain_vec, w_in, w_out, state):
    stored, hidden, active = state
    grad_branch = share_grads((0.5 * incoming).astype(jnp.bfloat16))
    grad_w_out = jnp.einsum("srf,srd->fd", active, grad_branch, preferred_element_type=jnp.float32)
    grad_active = jnp.einsum("srd,fd->srf", grad_branch, w_out, preferred_element_type=jnp.float32)
    sigmoid_vals = jax.nn.sigmoid(hidden)
    grad_hidden = (grad_active * sigmoid_vals * (1.0 + hidden * (1.0 - sigmoid_vals))).astype(
        jnp.bfloat16
    )
    grad_w_in = jnp.einsum("srd,srf->df", stored, grad_hidden, preferred_element_type=jnp.float32)
    grad_normed = backward_sum(((grad_hidden, w_in),))
    norm_value, norm_pull = jax.vjp(normed, residual, gain_vec)
    grad_residual, grad_gain = norm_pull(grad_normed)
    return (incoming + grad_residual, grad_gain, grad_w_in, grad_w_out)


def attention(residual, gain_vec, w_query, w_key, w_value, w_output, rel_table, segments):
    local_rows = normed(residual, gain_vec).astype(jnp.bfloat16)
    gathered = share_frames(local_rows)
    frames, row_count = (gathered.shape[0], gathered.shape[1])
    head_count = rel_table.shape[0]

    def project(weight):
        projected = jnp.einsum("srd,dc->src", gathered, weight, preferred_element_type=jnp.float32)
        return per_head(projected.astype(jnp.bfloat16), row_count, head_count)

    query_rows, key_rows, value_rows = (project(w_query), project(w_key), project(w_value))
    tables = jnp.tile(rel_table, (row_count, 1))
    labels = jnp.repeat(segments, head_count, axis=0)

    def one_head(record):
        query_head, key_head, value_head, table_row, label_row = record
        scores = head_scores(query_head, key_head, rel_band(table_row, frames), label_row)
        row_max = jnp.max(scores, axis=-1, keepdims=True)
        log_total = row_max + jnp.log(jnp.sum(jnp.exp(scores - row_max), axis=-1, keepdims=True))
        attend = jnp.exp(scores - log_total).astype(jnp.bfloat16)
        mixed = jnp.einsum("qk,kd->qd", attend, value_head, preferred_element_type=jnp.float32)
        return (mixed.astype(jnp.bfloat16), log_total[:, 0])

    attended, log_totals = lax.map(one_head, (query_rows, key_rows, value_rows, tables, labels))
    attended = per_frame(attended, row_count, head_count)
    branch = forward_sum(((attended, w_output),))
    return (residual + branch, (gathered, query_rows, key_rows, value_rows, attended, log_totals))


def attention_back(
    incoming, residual, gain_vec, w_query, w_key, w_value, w_output, rel_table, segments, state
):
    stored, query_rows, key_rows, value_rows, attended, log_totals = state
    frames, row_count = (stored.shape[0], stored.shape[1])
    head_count = rel_table.shape[0]
    grad_branch = share_grads(incoming.astype(jnp.bfloat16))
    grad_w_output = jnp.einsum(
        "src,srd->cd", attended, grad_branch, preferred_element_type=jnp.float32
    )
    grad_mixed = jnp.einsum(
        "srd,cd->src", grad_branch, w_output, preferred_element_type=jnp.float32
    )
    grad_mixed = per_head(grad_mixed.astype(jnp.bfloat16), row_count, head_count)
    tables = jnp.tile(rel_table, (row_count, 1))
    labels = jnp.repeat(segments, head_count, axis=0)

    def one_head(record):
        query_head, key_head, value_head, table_row, label_row, log_total, grad_head = record
        score_scale = query_head.shape[-1] ** (-0.5)
        rel_bias, band_pull = jax.vjp(lambda table_vals: rel_band(table_vals, frames), table_row)
        scores = head_scores(query_head, key_head, rel_bias, label_row)
        attend = jnp.exp(scores - log_total[:, None])
        grad_value = jnp.einsum(
            "qk,qd->kd", attend.astype(jnp.bfloat16), grad_head, preferred_element_type=jnp.float32
        )
        grad_attend = jnp.einsum(
            "qd,kd->qk", grad_head, value_head, preferred_element_type=jnp.float32
        )
        grad_scores = attend * (grad_attend - jnp.sum(attend * grad_attend, axis=-1, keepdims=True))
        grad_scores = grad_scores.astype(jnp.bfloat16)
        grad_query = (
            jnp.einsum("qk,kd->qd", grad_scores, key_head, preferred_element_type=jnp.float32)
            * score_scale
        )
        grad_key = (
            jnp.einsum("qk,qd->kd", grad_scores, query_head, preferred_element_type=jnp.float32)
            * score_scale
        )
        grad_table = band_pull(grad_scores.astype(jnp.float32))[0]
        return (
            grad_query.astype(jnp.bfloat16),
            grad_key.astype(jnp.bfloat16),
            grad_value.astype(jnp.bfloat16),
            grad_table,
        )

    grad_queries, grad_keys, grad_values, grad_tables = lax.map(
        one_head, (query_rows, key_rows, value_rows, tables, labels, log_totals, grad_mixed)
    )
    grad_queries = per_frame(grad_queries, row_count, head_count)
    grad_keys = per_frame(grad_keys, row_count, head_count)
    grad_values = per_frame(grad_values, row_count, head_count)
    grad_table = jnp.sum(grad_tables.reshape(row_count, head_count, grad_tables.shape[-1]), axis=0)
    stacked = jnp.stack([grad_queries, grad_keys, grad_values], axis=2)
    grad_projections = jnp.einsum(
        "srd,srtc->dtc", stored, stacked, preferred_element_type=jnp.float32
    )
    grad_normed = backward_sum(
        ((grad_queries, w_query), (grad_keys, w_key), (grad_values, w_value))
    )
    norm_value, norm_pull = jax.vjp(normed, residual, gain_vec)
    grad_residual, grad_gain = norm_pull(grad_normed)
    return (incoming + grad_residual, grad_gain, grad_table, grad_projections, grad_w_output)


def convolution(residual, gain_vec, w_glu, kernel, w_back, labels):
    local_rows = normed(residual, gain_vec).astype(jnp.bfloat16)
    gathered = share_frames(local_rows)
    channels = kernel.shape[1]
    glu_input = jnp.einsum(
        "srd,dc->src",
        gathered,
        w_glu.reshape(w_glu.shape[0], 2 * channels),
        preferred_element_type=jnp.float32,
    )
    active = gated_conv(glu_input, kernel, labels).astype(jnp.bfloat16)
    branch = forward_sum(((active, w_back),))
    return (residual + branch, (gathered, glu_input))


def convolution_back(incoming, residual, gain_vec, w_glu, kernel, w_back, labels, state):
    stored, glu_input = state
    channels = kernel.shape[1]
    width = w_glu.shape[0]
    glu_matrix = w_glu.reshape(width, 2 * channels)
    grad_branch = share_grads(incoming.astype(jnp.bfloat16))
    conv_value, conv_pull = jax.vjp(
        lambda glu_vals, taps: gated_conv(glu_vals, taps, labels), glu_input, kernel
    )
    active = conv_value.astype(jnp.bfloat16)
    grad_w_back = jnp.einsum("src,srd->cd", active, grad_branch, preferred_element_type=jnp.float32)
    grad_active = jnp.einsum("srd,cd->src", grad_branch, w_back, preferred_element_type=jnp.float32)
    grad_glu_input, grad_kernel = conv_pull(grad_active)
    grad_glu_input = grad_glu_input.astype(jnp.bfloat16)
    grad_w_glu = jnp.einsum(
        "srd,src->dc", stored, grad_glu_input, preferred_element_type=jnp.float32
    ).reshape(width, 2, channels)
    grad_normed = backward_sum(((grad_glu_input, glu_matrix),))
    norm_value, norm_pull = jax.vjp(normed, residual, gain_vec)
    grad_residual, grad_gain = norm_pull(grad_normed)
    return (incoming + grad_residual, grad_gain, grad_kernel, grad_w_glu, grad_w_back)


def shards(
    inputs,
    segments,
    cotangent,
    gain_one,
    first_in,
    first_out,
    gain_two,
    w_query,
    w_key,
    w_value,
    w_output,
    rel_table,
    gain_three,
    w_glu,
    kernel,
    w_back,
    gain_four,
    second_in,
    second_out,
    gain_five,
):
    frame_labels = segments.T
    start_frames = inputs.astype(jnp.float32)
    after_one, state_one = feed_forward(start_frames, gain_one, first_in, first_out)
    after_two, state_two = attention(
        after_one, gain_two, w_query, w_key, w_value, w_output, rel_table, segments
    )
    after_three, state_three = convolution(
        after_two, gain_three, w_glu, kernel, w_back, frame_labels
    )
    after_four, state_four = feed_forward(after_three, gain_four, second_in, second_out)
    final_rows, final_pull = jax.vjp(normed, after_four, gain_five)
    output = final_rows.astype(jnp.bfloat16)
    incoming, grad_five = final_pull(cotangent.astype(jnp.float32))
    incoming, grad_four, grad_second_in, grad_second_out = feed_back(
        incoming, after_three, gain_four, second_in, second_out, state_four
    )
    grad_second_in, grad_second_out = settle(grad_second_in, grad_second_out)
    incoming, grad_three, grad_kernel, grad_w_glu, grad_w_back = convolution_back(
        incoming, after_two, gain_three, w_glu, kernel, w_back, frame_labels, state_three
    )
    grad_w_glu, grad_w_back = settle(grad_w_glu, grad_w_back)
    incoming, grad_two, grad_table, grad_projections, grad_w_output = attention_back(
        incoming,
        after_one,
        gain_two,
        w_query,
        w_key,
        w_value,
        w_output,
        rel_table,
        segments,
        state_two,
    )
    grad_projections, grad_w_output = settle(grad_projections, grad_w_output)
    incoming, grad_one, grad_first_in, grad_first_out = feed_back(
        incoming, start_frames, gain_one, first_in, first_out, state_one
    )
    grad_first_in, grad_first_out = settle(grad_first_in, grad_first_out)
    grad_table, grad_kernel = lax.psum((grad_table, grad_kernel), "dp")
    grad_one, grad_two, grad_three, grad_four, grad_five = lax.psum(
        (grad_one, grad_two, grad_three, grad_four, grad_five), ("dp", "tensor")
    )
    return (
        output,
        incoming,
        grad_one,
        grad_first_in,
        grad_first_out,
        grad_two,
        grad_projections[:, 0],
        grad_projections[:, 1],
        grad_projections[:, 2],
        grad_w_output,
        grad_table,
        grad_three,
        grad_w_glu,
        grad_kernel,
        grad_w_back,
        grad_four,
        grad_second_in,
        grad_second_out,
        grad_five,
    )


def solution(mesh):
    in_specs = (
        P("tensor", "dp", None),
        P("dp", None),
        P("tensor", "dp", None),
        P(),
        P(None, "tensor"),
        P("tensor", None),
        P(),
        P(None, "tensor"),
        P(None, "tensor"),
        P(None, "tensor"),
        P("tensor", None),
        P("tensor", None),
        P(),
        P(None, None, "tensor"),
        P(None, "tensor"),
        P("tensor", None),
        P(),
        P(None, "tensor"),
        P("tensor", None),
        P(),
    )
    out_specs = (
        P("tensor", "dp", None),
        P("tensor", "dp", None),
        P(),
        P("dp", "tensor"),
        P("tensor", "dp"),
        P(),
        P("dp", "tensor"),
        P("dp", "tensor"),
        P("dp", "tensor"),
        P("tensor", "dp"),
        P("tensor", None),
        P(),
        P("dp", None, "tensor"),
        P(None, "tensor"),
        P("tensor", "dp"),
        P(),
        P("dp", "tensor"),
        P("tensor", "dp"),
        P(),
    )
    return jax.shard_map(shards, mesh=mesh, in_specs=in_specs, out_specs=out_specs, check_vma=False)
```

profile of v0, /device:TPU:0, one launch (start us, length us, event | category | flops | bytes accessed | tf_op | source)
XLA Modules:
  0.0 2913.9 jit_solution(12028822160477935282)
XLA Ops:
  20.7 48.4 %all-gather.9.cloned.1.call-done = bf16[1500,1,1024]{2,1,0:T(2,128)(2,1)} async-done(((bf16[375,1,1024]{2,1,0:T(2,128)(2,1)}), bf16[1500,1,1024]{2,1,0:T(2,128)(2,1)}) %all-gather.9.cloned.1.call-update) | async-done | bytes 3072016 | tf_op jit(solution)/shard_map/all_gather | solution.py:54
  83.4 30.9 %fusion = bf16[376,1024]{1,0:T(8,128)(2,1)S(1)} fusion(bf16[1500,1,1024]{2,0,1:T(8,128)(2,1)} %fusion.77), kind=kCustom, calls=%all-reduce-scatter | all-reduce-scatter fusion | flops 1540097 | bytes 3842560
  141.4 48.1 %all-gather.11.cloned.1.call-done = bf16[1500,1,1024]{2,1,0:T(2,128)(2,1)} async-done(((bf16[375,1,1024]{2,1,0:T(2,128)(2,1)}), bf16[1500,1,1024]{2,1,0:T(2,128)(2,1)}) %all-gather.11.cloned.1.call-update) | async-done | bytes 3072016 | tf_op jit(solution)/shard_map/all_gather | solution.py:54
  213.3 417.3 %while.32 = (s32[]{:T(128)}, bf16[4,1500,64]{1,2,0:T(8,128)(2,1)S(1)}, f32[4,1500]{1,0:T(4,128)S(1)}, s32[4,1500]{1,0:T(4,128)S(1)}, bf16[4,1500,64]{2,1,0:T(8,1...) while((s32[]{:T(128)}, ...), condition=%wide.region_8.9_spmd, body=%wide.region_5.8_spmd.sunk | while | flops 606376448 | bytes 199957408 | solution.py:172
  239.6 20.0 tile.35
  259.6 14.1 slice.666
  273.7 27.0 reshape.1090
  339.7 20.0 tile.35
  359.8 14.1 slice.666
  373.8 27.0 reshape.1090
  439.9 20.0 tile.35
  459.9 14.1 slice.666
  474.0 27.0 reshape.1090
  540.0 20.0 tile.35
  560.0 14.1 slice.666
  574.1 27.0 reshape.1090
  635.3 30.8 %fusion.1 = bf16[376,1024]{1,0:T(8,128)(2,1)S(1)} fusion(bf16[1500,1,1024]{2,0,1:T(8,128)(2,1)} %fusion.74), kind=kCustom, calls=%all-reduce-scatter.1 | all-reduce-scatter fusion | flops 1540097 | bytes 3842560
  689.4 46.0 %all-gather.13.cloned.1.call-done = bf16[1500,1,1024]{2,1,0:T(2,128)(2,1)} async-done(((bf16[375,1,1024]{2,1,0:T(2,128)(2,1)}), bf16[1500,1,1024]{2,1,0:T(2,128)(2,1)}) %all-gather.13.cloned.1.call-update) | async-done | bytes 3072016 | tf_op jit(solution)/shard_map/all_gather | solution.py:54
  741.9 12.0 select_add_fusion
  757.6 31.5 %fusion.2 = bf16[376,1024]{1,0:T(8,128)(2,1)} fusion(bf16[1500,1,1024]{2,0,1:T(8,128)(2,1)} %fusion.75), kind=kCustom, calls=%all-reduce-scatter.2 | all-reduce-scatter fusion | flops 1540097 | bytes 3842560
  815.9 49.6 %all-gather.15.cloned.1.call-done = bf16[1500,1,1024]{2,1,0:T(2,128)(2,1)} async-done(((bf16[375,1,1024]{2,1,0:T(2,128)(2,1)}), bf16[1500,1,1024]{2,1,0:T(2,128)(2,1)}) %all-gather.15.cloned.1.call-update) | async-done | bytes 3072016 | tf_op jit(solution)/shard_map/all_gather | solution.py:54
  880.0 30.8 %fusion.3 = bf16[376,1024]{1,0:T(8,128)(2,1)S(1)} fusion(bf16[1500,1,1024]{2,0,1:T(8,128)(2,1)} %fusion.78), kind=kCustom, calls=%all-reduce-scatter.3 | all-reduce-scatter fusion | flops 1540097 | bytes 3842560
  945.4 49.6 %all-gather.17.cloned.1.call-done = bf16[1500,1,1024]{2,1,0:T(2,128)(2,1)} async-done(((bf16[375,1,1024]{2,1,0:T(2,128)(2,1)}), bf16[1500,1,1024]{2,1,0:T(2,128)(2,1)}) %all-gather.17.cloned.1.call-update) | async-done | bytes 3072016 | tf_op jit(solution)/shard_map/all_gather | solution.py:58
  1010.9 30.8 %fusion.4 = bf16[376,1024]{1,0:T(8,128)(2,1)S(1)} fusion(bf16[1500,1,1024]{2,0,1:T(8,128)(2,1)} %fusion.79), kind=kCustom, calls=%all-reduce-scatter.4 | all-reduce-scatter fusion | flops 1540097 | bytes 3842560
  1067.4 49.6 %all-gather.19.cloned.1.call-done = bf16[1500,1,1024]{2,1,0:T(2,128)(2,1)} async-done(((bf16[375,1,1024]{2,1,0:T(2,128)(2,1)}), bf16[1500,1,1024]{2,1,0:T(2,128)(2,1)}) %all-gather.19.cloned.1.call-update) | async-done | bytes 3072016 | tf_op jit(solution)/shard_map/all_gather | solution.py:58
  1117.0 15.2 multiply_reduce_fusion.12
  1132.2 15.3 multiply_reduce_fusion.16
  1164.2 11.7 pad_add_fusion
  1185.5 30.8 %fusion.5 = bf16[376,1024]{1,0:T(8,128)(2,1)S(1)} fusion(bf16[1500,1,1024]{2,0,1:T(8,128)(2,1)} %fusion.73), kind=kCustom, calls=%all-reduce-scatter.5 | all-reduce-scatter fusion | flops 1540097 | bytes 3842560
  1242.2 49.6 %all-gather.21.cloned.1.call-done = bf16[1500,1,1024]{2,1,0:T(2,128)(2,1)} async-done(((bf16[375,1,1024]{2,1,0:T(2,128)(2,1)}), bf16[1500,1,1024]{2,1,0:T(2,128)(2,1)}) %all-gather.21.cloned.1.call-update) | async-done | bytes 3072016 | tf_op jit(solution)/shard_map/all_gather | solution.py:58
  1298.9 841.6 %while.33 = (s32[]{:T(128)}, bf16[4,1500,64]{1,2,0:T(8,128)(2,1)}, bf16[4,1500,64]{1,2,0:T(8,128)(2,1)}, bf16[4,1500,64]{1,2,0:T(8,128)(2,1)}, f32[4,257]{1,0:T(...) while((s32[]{:T(128)}, bf16[4,1500,64]{1,2,0:T(8,128)(2,1)}, ...), condition=%wide.region_29.30_spmd, body=%wide.region_26.29_spmd.sunk | while | flops 1494280448 | bytes 381868960 | solution.py:225
  1314.9 20.0 tile.37
  1335.0 14.0 slice.668
  1349.0 27.7 reshape.1092
  1444.2 23.3 reshape.1093
  1478.8 20.2 reshape.1094
  1523.7 20.0 tile.37
  1543.7 14.0 slice.668
  1557.8 27.7 reshape.1092
  1653.0 23.1 reshape.1093
  1676.2 11.2 pad_convert_fusion.2
  1687.4 20.2 reshape.1094
  1732.5 20.0 tile.37
  1752.5 14.0 slice.668
  1766.5 27.6 reshape.1092
  1861.7 23.1 reshape.1093
  1884.9 11.2 pad_convert_fusion.2
  1896.1 20.2 reshape.1094
  1941.2 20.0 tile.37
  1961.2 14.0 slice.668
  1975.3 27.6 reshape.1092
  2070.4 23.1 reshape.1093
  2104.8 20.2 reshape.1094
  2147.9 30.8 %fusion.6 = bf16[376,1024]{1,0:T(8,128)(2,1)S(1)} fusion(bf16[1500,1,1024]{2,0,1:T(8,128)(2,1)} %fusion.76), kind=kCustom, calls=%all-reduce-scatter.6 | all-reduce-scatter fusion | flops 1540097 | bytes 3842560
  2295.8 14.9 multiply_reduce_fusion.22
  2321.6 33.9 %fusion.7 = bf16[376,1024]{1,0:T(8,128)(2,1)S(1)} fusion(bf16[1500,1,1024]{2,0,1:T(8,128)(2,1)} %fusion.80), kind=kCustom, calls=%all-reduce-scatter.7 | all-reduce-scatter fusion | flops 1540097 | bytes 3842560
  2359.0 38.5 %all-reduce.85 = (f32[4,257]{1,0:T(4,128)}, f32[31,256]{1,0:T(8,128)}) all-reduce(f32[4,257]{1,0:T(4,128)S(1)} %get-tuple-element.278, f32[31,256]{1,0:T(8,128)S(1)} %pad_add_fusion.7), channel_id=1, replica_groups=mesh['dp'=8,'tensor'=4] {'dp'}, use_global_device_ids=true, to_apply=%region_44.45 | all-reduce | flops 8964 | bytes 71712 | tf_op jit(solution)/shard_map/psum | solution.py:342
  2410.1 39.0 %all-reduce.84 = (f32[1024]{0:T(1024)}, f32[1024]{0:T(1024)}, f32[1024]{0:T(1024)}, f32[1024]{0:T(1024)}, f32[1024]{0:T(1024)}) all-reduce(f32[1024]{0:T(1024)S(1)} %get-tuple-element.454, f32[1024]{0:T(1024)S(1)} %get-tuple-element.452, f32[1024]{0:T(1024)S(1)} %copy-done.103, ...), channel_id=1, replica_groups=mesh['dp'=8,'tensor'=4] {'dp','tensor'}, use_global_device_ids=true, to_apply=%region_37.38 | all-reduce | flops 5120 | bytes 40960 | tf_op jit(solution)/shard_map/psum | solution.py:343
  2460.0 11.7 reduce-scatter.43.cloned.1.call-done
  2471.6 91.5 %reduce-scatter.45.cloned.1.call-done = f32[128,1024]{1,0:T(8,128)} async-done(((f32[1024,1024]{1,0:T(8,128)}), f32[128,1024]{1,0:T(8,128)}) %reduce-scatter.45.cloned.1.call-update) | async-done | bytes 524304 | tf_op jit(solution)/shard_map/reduce_scatter | solution.py:89
  2563.1 92.5 %reduce-scatter.47.cloned.1.call-done = f32[1024,128]{1,0:T(8,128)} async-done(((f32[1024,1024]{1,0:T(8,128)}), f32[1024,128]{1,0:T(8,128)}) %reduce-scatter.47.cloned.1.call-update) | async-done | bytes 524304 | tf_op jit(solution)/shard_map/reduce_scatter | solution.py:90
  2655.6 67.8 %reduce-scatter.39.cloned.1.call-done = f32[256,128]{1,0:T(8,128)} async-done(((f32[256,1024]{1,0:T(8,128)}), f32[256,128]{1,0:T(8,128)}) %reduce-scatter.39.cloned.1.call-update) | async-done | bytes 131088 | tf_op jit(solution)/shard_map/reduce_scatter | solution.py:90
  2723.4 91.0 %reduce-scatter.33.cloned.1.call-done = f32[128,1024]{1,0:T(8,128)} async-done(((f32[1024,1024]{1,0:T(8,128)}), f32[128,1024]{1,0:T(8,128)}) %reduce-scatter.33.cloned.1.call-update) | async-done | bytes 524304 | tf_op jit(solution)/shard_map/reduce_scatter | solution.py:89
  2814.4 92.8 %reduce-scatter.35.cloned.1.call-done = f32[1024,128]{1,0:T(8,128)} async-done(((f32[1024,1024]{1,0:T(8,128)}), f32[1024,128]{1,0:T(8,128)}) %reduce-scatter.35.cloned.1.call-update) | async-done | bytes 524304 | tf_op jit(solution)/shard_map/reduce_scatter | solution.py:90
  (579 shorter events, 999.8 us)
Async XLA Ops:
  7.2 868.1 %copy-start = (bf16[1024,1024]{1,0:T(8,128)(2,1)S(1)}, bf16[1024,1024]{1,0:T(8,128)(2,1)}, u32[]{:S(2)}) copy-start(bf16[1024,1024]{1,0:T(8,128)(2,1)} %param.42) | copy-start | bytes 6291460
  7.2 61.8 %all-gather.9.cloned.1.call-start = ((), (), s32[]{:S(2)}) async-start(), calls=%async_computation.8 | async-start | bytes 7680000 | tf_op jit(solution)/shard_map/all_gather | solution.py:54
  20.6 168.9 %all-gather.11.cloned.1.call-start = ((), (), s32[]{:S(2)}) async-start(), calls=%async_computation.9 | async-start | bytes 7680000 | tf_op jit(solution)/shard_map/all_gather | solution.py:54
  83.4 32.7 %copy-start.118 = (u32[32]{0:T(128)S(1)}, u32[32]{0:T(128)}, u32[]{:S(2)}) copy-start(u32[32]{0:T(128)} %constant.348) | copy-start | bytes 388
  114.4 2.9 collective-permute-start
  140.7 594.7 %all-gather.13.cloned.1.call-start = ((), (), s32[]{:S(2)}) async-start(), calls=%async_computation.10 | async-start | bytes 7680000 | tf_op jit(solution)/shard_map/all_gather | solution.py:54
  141.4 53.7 %copy-start.42 = (bf16[1024,256]{1,0:T(8,128)(2,1)S(1)}, bf16[1024,256]{1,0:T(8,128)(2,1)}, u32[]{:S(2)}) copy-start(bf16[1024,256]{1,0:T(8,128)(2,1)} %param.32) | copy-start | bytes 1572868
  666.1 2.1 collective-permute-start.1
  685.8 179.7 %all-gather.15.cloned.1.call-start = ((), (), s32[]{:S(2)}) async-start(), calls=%async_computation.11 | async-start | bytes 7680000 | tf_op jit(solution)/shard_map/all_gather | solution.py:54
  688.5 459.1 %copy-start.86 = (pred[1500]{0:T(1024)(128)(4,1)}, pred[1500]{0:T(1024)(128)(4,1)S(1)}, u32[]{:S(2)}) copy-start(pred[1500]{0:T(1024)(128)(4,1)S(1)} %get-tuple-element.483) | copy-start | bytes 4504
  688.5 463.0 %copy-start.60 = (pred[1500]{0:T(1024)(128)(4,1)}, pred[1500]{0:T(1024)(128)(4,1)S(1)}, u32[]{:S(2)}) copy-start(pred[1500]{0:T(1024)(128)(4,1)S(1)} %get-tuple-element.484) | copy-start | bytes 4504
  688.5 468.8 %copy-start.62 = (pred[1500]{0:T(1024)(128)(4,1)}, pred[1500]{0:T(1024)(128)(4,1)S(1)}, u32[]{:S(2)}) copy-start(pred[1500]{0:T(1024)(128)(4,1)S(1)} %get-tuple-element.485) | copy-start | bytes 4504
  688.7 462.7 %copy-start.74 = (pred[1500]{0:T(1024)(128)(4,1)}, pred[1500]{0:T(1024)(128)(4,1)S(1)}, u32[]{:S(2)}) copy-start(pred[1500]{0:T(1024)(128)(4,1)S(1)} %get-tuple-element.471) | copy-start | bytes 4504
  688.8 462.7 %copy-start.76 = (pred[1500]{0:T(1024)(128)(4,1)}, pred[1500]{0:T(1024)(128)(4,1)S(1)}, u32[]{:S(2)}) copy-start(pred[1500]{0:T(1024)(128)(4,1)S(1)} %get-tuple-element.472) | copy-start | bytes 4504
  688.8 462.7 %copy-start.78 = (pred[1500]{0:T(1024)(128)(4,1)}, pred[1500]{0:T(1024)(128)(4,1)S(1)}, u32[]{:S(2)}) copy-start(pred[1500]{0:T(1024)(128)(4,1)S(1)} %get-tuple-element.473) | copy-start | bytes 4504
  688.8 468.5 %copy-start.68 = (pred[1500]{0:T(1024)(128)(4,1)}, pred[1500]{0:T(1024)(128)(4,1)S(1)}, u32[]{:S(2)}) copy-start(pred[1500]{0:T(1024)(128)(4,1)S(1)} %get-tuple-element.468) | copy-start | bytes 4504
  688.8 468.5 %copy-start.70 = (pred[1500]{0:T(1024)(128)(4,1)}, pred[1500]{0:T(1024)(128)(4,1)S(1)}, u32[]{:S(2)}) copy-start(pred[1500]{0:T(1024)(128)(4,1)S(1)} %get-tuple-element.469) | copy-start | bytes 4504
  688.8 468.5 %copy-start.72 = (pred[1500]{0:T(1024)(128)(4,1)}, pred[1500]{0:T(1024)(128)(4,1)S(1)}, u32[]{:S(2)}) copy-start(pred[1500]{0:T(1024)(128)(4,1)S(1)} %get-tuple-element.470) | copy-start | bytes 4504
  689.0 458.5 %copy-start.88 = (pred[1500]{0:T(1024)(128)(4,1)}, pred[1500]{0:T(1024)(128)(4,1)S(1)}, u32[]{:S(2)}) copy-start(pred[1500]{0:T(1024)(128)(4,1)S(1)} %get-tuple-element.479) | copy-start | bytes 4504
  689.1 458.5 %copy-start.90 = (pred[1500]{0:T(1024)(128)(4,1)}, pred[1500]{0:T(1024)(128)(4,1)S(1)}, u32[]{:S(2)}) copy-start(pred[1500]{0:T(1024)(128)(4,1)S(1)} %get-tuple-element.480) | copy-start | bytes 4504
  689.1 458.5 %copy-start.92 = (pred[1500]{0:T(1024)(128)(4,1)}, pred[1500]{0:T(1024)(128)(4,1)S(1)}, u32[]{:S(2)}) copy-start(pred[1500]{0:T(1024)(128)(4,1)S(1)} %get-tuple-element.481) | copy-start | bytes 4504
  689.1 458.5 %copy-start.94 = (pred[1500]{0:T(1024)(128)(4,1)}, pred[1500]{0:T(1024)(128)(4,1)S(1)}, u32[]{:S(2)}) copy-start(pred[1500]{0:T(1024)(128)(4,1)S(1)} %get-tuple-element.482) | copy-start | bytes 4504
  689.1 462.4 %copy-start.64 = (pred[1500]{0:T(1024)(128)(4,1)}, pred[1500]{0:T(1024)(128)(4,1)S(1)}, u32[]{:S(2)}) copy-start(pred[1500]{0:T(1024)(128)(4,1)S(1)} %get-tuple-element.477) | copy-start | bytes 4504
  689.1 462.4 %copy-start.66 = (pred[1500]{0:T(1024)(128)(4,1)}, pred[1500]{0:T(1024)(128)(4,1)S(1)}, u32[]{:S(2)}) copy-start(pred[1500]{0:T(1024)(128)(4,1)S(1)} %get-tuple-element.478) | copy-start | bytes 4504
  689.1 462.4 %copy-start.80 = (pred[1500]{0:T(1024)(128)(4,1)}, pred[1500]{0:T(1024)(128)(4,1)S(1)}, u32[]{:S(2)}) copy-start(pred[1500]{0:T(1024)(128)(4,1)S(1)} %get-tuple-element.474) | copy-start | bytes 4504
  689.1 462.4 %copy-start.82 = (pred[1500]{0:T(1024)(128)(4,1)}, pred[1500]{0:T(1024)(128)(4,1)S(1)}, u32[]{:S(2)}) copy-start(pred[1500]{0:T(1024)(128)(4,1)S(1)} %get-tuple-element.475) | copy-start | bytes 4504
  689.1 462.4 %copy-start.84 = (pred[1500]{0:T(1024)(128)(4,1)}, pred[1500]{0:T(1024)(128)(4,1)S(1)}, u32[]{:S(2)}) copy-start(pred[1500]{0:T(1024)(128)(4,1)S(1)} %get-tuple-element.476) | copy-start | bytes 4504
  789.9 2.1 collective-permute-start.2
  815.9 179.2 %all-gather.17.cloned.1.call-start = ((), (), s32[]{:S(2)}) async-start(), calls=%async_computation.12 | async-start | bytes 7680000 | tf_op jit(solution)/shard_map/all_gather | solution.py:58
  910.9 2.1 collective-permute-start.3
  945.4 171.6 %all-gather.19.cloned.1.call-start = ((), (), s32[]{:S(2)}) async-start(), calls=%async_computation.13 | async-start | bytes 7680000 | tf_op jit(solution)/shard_map/all_gather | solution.py:58
  1041.8 2.2 collective-permute-start.4
  1067.3 49.7 %copy-start.123 = (bf16[256,1024]{1,0:T(8,128)(2,1)S(1)}, bf16[256,1024]{1,0:T(8,128)(2,1)}, u32[]{:S(2)}) copy-start(bf16[256,1024]{1,0:T(8,128)(2,1)} %param.39) | copy-start | bytes 1572868
  1067.4 224.4 %all-gather.21.cloned.1.call-start = ((), (), s32[]{:S(2)}) async-start(), calls=%async_computation.14 | async-start | bytes 7680000 | tf_op jit(solution)/shard_map/all_gather | solution.py:58
  1132.2 25.1 copy-start.3
  1216.4 2.2 collective-permute-start.5
  1242.2 49.7 %copy-start.124 = (bf16[256,1024]{1,0:T(8,128)(2,1)S(1)}, bf16[256,1024]{1,0:T(8,128)(2,1)}, u32[]{:S(2)}) copy-start(bf16[256,1024]{1,0:T(8,128)(2,1)} %param.34) | copy-start | bytes 1572868
  1242.2 1020.0 %all-gather.23.cloned.1.call-start = ((), (), s32[]{:S(2)}) async-start(), calls=%async_computation.15 | async-start | bytes 7680000 | tf_op jit(solution)/shard_map/all_gather | solution.py:58
  1298.9 841.6 %copy-start.43 = (bf16[1024,256]{1,0:T(8,128)(2,1)S(1)}, bf16[1024,256]{1,0:T(8,128)(2,1)}, u32[]{:S(2)}) copy-start(bf16[1024,256]{1,0:T(8,128)(2,1)} %param.32) | copy-start | bytes 1572868
  2179.6 2.2 collective-permute-start.6
  2205.8 151.3 %reduce-scatter.41.cloned.1.call-start = ((), (), s32[]{:S(2)}) async-start(), calls=%async_computation.20 | async-start | bytes 2359296 | tf_op jit(solution)/shard_map/reduce_scatter | solution.py:89
  2219.8 238.4 %reduce-scatter.37.cloned.1.call-start = ((), (), s32[]{:S(2)}) async-start(), calls=%async_computation.18 | async-start | bytes 3538944 | tf_op jit(solution)/shard_map/reduce_scatter | solution.py:89
  2229.2 242.4 %reduce-scatter.43.cloned.1.call-start = ((), (), s32[]{:S(2)}) async-start(), calls=%async_computation.21 | async-start | bytes 1179648 | tf_op jit(solution)/shard_map/reduce_scatter | solution.py:90
  2235.9 327.3 %reduce-scatter.45.cloned.1.call-start = ((), (), s32[]{:S(2)}) async-start(), calls=%async_computation.22 | async-start | bytes 4718592 | tf_op jit(solution)/shard_map/reduce_scatter | solution.py:89
  2245.6 410.0 %reduce-scatter.47.cloned.1.call-start = ((), (), s32[]{:S(2)}) async-start(), calls=%async_computation.23 | async-start | bytes 4718592 | tf_op jit(solution)/shard_map/reduce_scatter | solution.py:90
  2256.1 467.3 %reduce-scatter.39.cloned.1.call-start = ((), (), s32[]{:S(2)}) async-start(), calls=%async_computation.19 | async-start | bytes 1179648 | tf_op jit(solution)/shard_map/reduce_scatter | solution.py:90
  2262.1 552.3 %reduce-scatter.33.cloned.1.call-start = ((), (), s32[]{:S(2)}) async-start(), calls=%async_computation.16 | async-start | bytes 4718592 | tf_op jit(solution)/shard_map/reduce_scatter | solution.py:89
  2282.0 625.2 %reduce-scatter.35.cloned.1.call-start = ((), (), s32[]{:S(2)}) async-start(), calls=%async_computation.17 | async-start | bytes 4718592 | tf_op jit(solution)/shard_map/reduce_scatter | solution.py:90
  2321.5 35.3 %copy-start.105 = (f32[256]{0:T(256)S(1)}, f32[256]{0:T(256)}, u32[]{:S(2)}) copy-start(f32[256]{0:T(256)} %get-tuple-element.433) | copy-start | bytes 3076
  2321.5 35.3 %copy-start.106 = (f32[256]{0:T(256)S(1)}, f32[256]{0:T(256)}, u32[]{:S(2)}) copy-start(f32[256]{0:T(256)} %get-tuple-element.434) | copy-start | bytes 3076
  2321.5 35.3 %copy-start.107 = (f32[256]{0:T(256)S(1)}, f32[256]{0:T(256)}, u32[]{:S(2)}) copy-start(f32[256]{0:T(256)} %get-tuple-element.435) | copy-start | bytes 3076
  2321.5 35.4 %copy-start.108 = (f32[256]{0:T(256)S(1)}, f32[256]{0:T(256)}, u32[]{:S(2)}) copy-start(f32[256]{0:T(256)} %get-tuple-element.436) | copy-start | bytes 3076
  2321.5 35.4 %copy-start.109 = (f32[256]{0:T(256)S(1)}, f32[256]{0:T(256)}, u32[]{:S(2)}) copy-start(f32[256]{0:T(256)} %get-tuple-element.437) | copy-start | bytes 3076
  2321.5 35.4 %copy-start.110 = (f32[256]{0:T(256)S(1)}, f32[256]{0:T(256)}, u32[]{:S(2)}) copy-start(f32[256]{0:T(256)} %get-tuple-element.438) | copy-start | bytes 3076
  2321.6 35.4 %copy-start.111 = (f32[256]{0:T(256)S(1)}, f32[256]{0:T(256)}, u32[]{:S(2)}) copy-start(f32[256]{0:T(256)} %get-tuple-element.439) | copy-start | bytes 3076
  2321.6 35.4 %copy-start.112 = (f32[256]{0:T(256)S(1)}, f32[256]{0:T(256)}, u32[]{:S(2)}) copy-start(f32[256]{0:T(256)} %get-tuple-element.440) | copy-start | bytes 3076
  2321.6 35.4 %copy-start.113 = (f32[256]{0:T(256)S(1)}, f32[256]{0:T(256)}, u32[]{:S(2)}) copy-start(f32[256]{0:T(256)} %get-tuple-element.441) | copy-start | bytes 3076
  2321.6 35.4 %copy-start.114 = (f32[256]{0:T(256)S(1)}, f32[256]{0:T(256)}, u32[]{:S(2)}) copy-start(f32[256]{0:T(256)} %get-tuple-element.442) | copy-start | bytes 3076
  2321.6 35.4 %copy-start.115 = (f32[256]{0:T(256)S(1)}, f32[256]{0:T(256)}, u32[]{:S(2)}) copy-start(f32[256]{0:T(256)} %get-tuple-element.443) | copy-start | bytes 3076
  2321.6 35.4 %copy-start.116 = (f32[256]{0:T(256)S(1)}, f32[256]{0:T(256)}, u32[]{:S(2)}) copy-start(f32[256]{0:T(256)} %get-tuple-element.444) | copy-start | bytes 3076
  2321.6 35.4 %copy-start.117 = (f32[256]{0:T(256)S(1)}, f32[256]{0:T(256)}, u32[]{:S(2)}) copy-start(f32[256]{0:T(256)} %get-tuple-element.445) | copy-start | bytes 3076
  2355.6 41.9 %collective-permute-start.7 = (bf16[3,1024]{1,0:T(4,128)(2,1)S(1)}, bf16[3,1024]{1,0:T(4,128)(2,1)S(1)}, u32[]{:S(2)}, u32[]{:S(2)}) collective-permute-start(bf16[3,1024]{1,0:T(4,128)(2,1)S(1)} %slice.522), channel_id=1, source_target_pairs={{0,1},{1,2},{2,3},{4,5},{5,6},{6,7},{8,9},{9,10},{10,11},{12,13},{... | collective-permute-start | bytes 18440
  2403.8 45.3 %copy-start.98 = (f32[375]{0:T(512)S(1)}, f32[375]{0:T(512)}, u32[]{:S(2)}) copy-start(f32[375]{0:T(512)} %copy-done.97) | copy-start | bytes 4504
  2455.3 451.9 %copy-start.1 = (bf16[1024,1024]{1,0:T(8,128)(2,1)S(1)}, bf16[1024,1024]{1,0:T(8,128)(2,1)}, u32[]{:S(2)}) copy-start(bf16[1024,1024]{1,0:T(8,128)(2,1)} %param.42) | copy-start | bytes 6291460
  (93 other events, 503.2 us)
Sparse Core Ops, SparseCore 0:
  20.7 48.2 all-gather.8
  140.9 48.6 all-gather.10
  686.0 49.4 all-gather.12
  816.0 49.4 all-gather.14
  945.5 49.4 all-gather.16
  1067.5 49.4 all-gather.18
  1242.3 49.4 all-gather.20
  2205.9 49.4 all-gather.22
  2258.9 67.8 reduce-scatter.40
  2330.3 74.2 reduce-scatter.36
  2408.6 62.9 reduce-scatter.42
  2476.1 86.9 reduce-scatter.44
  2567.3 88.2 reduce-scatter.46
  2659.8 63.5 reduce-scatter.38
  2727.5 86.9 reduce-scatter.32
  2818.9 88.2 reduce-scatter.34
where the time goes:
time: 2930 us; the launch traced here: 2910 us
  local copies, waits for them, and re-layouts  1070 us (37%)
  waiting for transfers between devices  793 us (27%)
  other arithmetic  347 us (12%)
  blocking collectives  328 us (11%)
  matrix products  324 us (11%)
    reshape x12, local copies, waits for them, and re-layouts, rel_band(): return tiled.reshape(frames, 2 * frames - 1)[:, frames - 1:]  311 us
    reduce_scatter x4, waiting for transfers between devices, settle(): lax.psum_scatter(grad_out, 'dp', scatter_dimension=1, tiled=True)  265 us
    unnamed x8, blocking collectives  250 us
    another operation x16, local copies, waits for them, and re-layouts, rel_band(): tiled = jnp.tile(diagonal_vals, frames)[:frames * (2 * frames - 1)]  229 us
    all_gather x4, waiting for transfers between devices, share_frames(): return lax.all_gather(local_rows, 'tensor', axis=0, tiled=True)  192 us
    reduce_scatter x4, waiting for transfers between devices, settle(): lax.psum_scatter(grad_in, 'dp', scatter_dimension=0, tiled=True)  183 us
    all_gather x4, waiting for transfers between devices, share_grads(): return lax.all_gather(local_rows, 'tensor', axis=0, tiled=True)  149 us
    slice x8, local copies, waits for them, and re-layouts, rel_band(): tiled = jnp.tile(diagonal_vals, frames)[:frames * (2 * frames - 1)]  112 us
  transfers between devices with their start and end apart: 24, of which 19 were waited for; matrix products, arithmetic and copies ran while one was open for 6% of the time, Pallas kernels for 0%

commit v1 on v0

--- a/solution.py
+++ b/solution.py
@@ -4,6 +4,28 @@
 from jax.sharding import PartitionSpec as P
 
 masked_score = -1e30
+
+
+def in_order(blocks, dim):
+    shape = list(blocks.shape[1:])
+    shape[dim] *= blocks.shape[0]
+    return jnp.moveaxis(blocks, 0, dim).reshape(shape)
+
+
+def collect(value, axis, dim):
+    size = lax.axis_size(axis)
+    pairs = [(i, (i + 1) % size) for i in range(size)]
+    back = [(b, a) for a, b in pairs]
+    lower, upper = ([], [])
+    for turn in range(size - 1):
+        if turn % 2 == 0:
+            lower.append(lax.ppermute(lower[-1] if lower else value, axis, pairs))
+        else:
+            upper.append(lax.ppermute(upper[-1] if upper else value, axis, back))
+    blocks = jnp.stack([*lower[::-1], value, *upper])
+    shift = lax.axis_index(axis) - len(lower)
+    blocks = blocks[(jnp.arange(size) - shift) % size]
+    return in_order(blocks, dim)
 
 
 def normed(residual, gain_vec):
@@ -51,7 +73,7 @@
 
 
 def share_frames(local_rows):
-    return lax.all_gather(local_rows, "tensor", axis=0, tiled=True)
+    return collect(local_rows, "tensor", 0)
 
 
 def share_grads(local_rows):

time: 2930 us -> 2800 us (0.956)
  other arithmetic: 347 us -> 247 us
  waiting for transfers between devices: 793 us -> 696 us
  local copies, waits for them, and re-layouts: 1070 us -> 1100 us
    all_gather x4 -> x0, waiting for transfers between devices: 192 us -> none  [share_frames(): return lax.all_gather(local_rows, 'tensor', axis=0, tiled=True)]
    ppermute x0 -> x12, waiting for transfers between devices: none -> 83.4 us  [the longest x8 83.4 us: collect(): lower.append(lax.ppermute(lower[-1] if lower else value, axis, pairs))]
    reduce_sum x5 -> x2, other arithmetic: 31.6 us -> 2.21 us  [normed(): centred = residual - row_mean]
    unnamed x287 -> x300, local copies, waits for them, and re-layouts: 92.9 us -> 65.9 us
  transfers between devices with their start and end apart: 24 -> 32, of which waited for: 19 -> 23; matrix products, arithmetic and copies ran while one was open for 6% -> 6% of each run, Pallas kernels for 0% -> 0%
where the time goes in v1:
time: 2800 us; the launch traced here: 2780 us
  local copies, waits for them, and re-layouts  1100 us (39%)
  waiting for transfers between devices  696 us (25%)
  blocking collectives  344 us (12%)
  matrix products  314 us (11%)
  other arithmetic  247 us (9%)
  starting transfers between devices  39.6 us (1%)
    reshape x12, local copies, waits for them, and re-layouts, rel_band(): return tiled.reshape(frames, 2 * frames - 1)[:, frames - 1:]  311 us
    reduce_scatter x4, waiting for transfers between devices, settle(): lax.psum_scatter(grad_out, 'dp', scatter_dimension=1, tiled=True)  275 us
    unnamed x8, blocking collectives  266 us
    another operation x16, local copies, waits for them, and re-layouts, rel_band(): tiled = jnp.tile(diagonal_vals, frames)[:frames * (2 * frames - 1)]  229 us
    reduce_scatter x4, waiting for transfers between devices, settle(): lax.psum_scatter(grad_in, 'dp', scatter_dimension=0, tiled=True)  184 us
    all_gather x4, waiting for transfers between devices, share_grads(): return lax.all_gather(local_rows, 'tensor', axis=0, tiled=True)  148 us
    slice x8, local copies, waits for them, and re-layouts, rel_band(): tiled = jnp.tile(diagonal_vals, frames)[:frames * (2 * frames - 1)]  112 us
    while x20, local copies, waits for them, and re-layouts  103 us
  transfers between devices with their start and end apart: 32, of which 23 were waited for; matrix products, arithmetic and copies ran while one was open for 6% of the time, Pallas kernels for 0%

profile of v1, /device:TPU:0, one launch (start us, length us, event | category | flops | bytes accessed | tf_op | source)
XLA Modules:
  0.0 2778.7 jit_solution(1136383429245849540)
XLA Ops:
  14.4 15.4 collective-permute-done
  66.6 34.7 %fusion = bf16[376,1024]{1,0:T(8,128)(2,1)} fusion(bf16[1500,1,1024]{2,0,1:T(8,128)(2,1)} %fusion.77), kind=kCustom, calls=%all-reduce-scatter | all-reduce-scatter fusion | flops 1540097 | bytes 3842560
  117.0 13.0 collective-permute-done.3
  174.7 417.1 %while.32 = (s32[]{:T(128)}, bf16[4,1500,64]{1,2,0:T(8,128)(2,1)S(1)}, f32[4,1500]{1,0:T(4,128)S(1)}, s32[4,1500]{1,0:T(4,128)S(1)}, bf16[4,1500,64]{2,1,0:T(8,1...) while((s32[]{:T(128)}, ...), condition=%wide.region_8.9_spmd, body=%wide.region_5.8_spmd.sunk | while | flops 606376448 | bytes 199957408 | solution.py:194
  200.8 20.0 tile.35
  220.8 14.0 slice.674
  234.9 27.0 reshape.1197
  300.9 20.0 tile.35
  320.9 14.0 slice.674
  335.0 27.0 reshape.1197
  401.0 20.0 tile.35
  421.0 14.0 slice.674
  435.1 27.0 reshape.1197
  501.1 20.0 tile.35
  521.2 14.0 slice.674
  535.2 27.0 reshape.1197
  595.8 35.8 %fusion.1 = bf16[376,1024]{1,0:T(8,128)(2,1)} fusion(bf16[1500,1,1024]{2,0,1:T(8,128)(2,1)} %fusion.74), kind=kCustom, calls=%all-reduce-scatter.1 | all-reduce-scatter fusion | flops 1540097 | bytes 3842560
  646.6 11.4 collective-permute-done.6
  687.4 11.9 select_add_fusion
  703.1 35.5 %fusion.2 = bf16[376,1024]{1,0:T(8,128)(2,1)S(1)} fusion(bf16[1500,1,1024]{2,0,1:T(8,128)(2,1)} %fusion.75), kind=kCustom, calls=%all-reduce-scatter.2 | all-reduce-scatter fusion | flops 1540097 | bytes 3842560
  750.9 13.2 collective-permute-done.9
  800.6 34.4 %fusion.3 = bf16[376,1024]{1,0:T(8,128)(2,1)S(1)} fusion(bf16[1500,1,1024]{2,0,1:T(8,128)(2,1)} %fusion.78), kind=kCustom, calls=%all-reduce-scatter.3 | all-reduce-scatter fusion | flops 1540097 | bytes 3842560
  851.6 49.1 %all-gather.5.cloned.1.call-done = bf16[1500,1,1024]{2,1,0:T(2,128)(2,1)} async-done(((bf16[375,1,1024]{2,1,0:T(2,128)(2,1)}), bf16[1500,1,1024]{2,1,0:T(2,128)(2,1)}) %all-gather.5.cloned.1.call-update) | async-done | bytes 3072016 | tf_op jit(solution)/shard_map/all_gather | solution.py:80
  916.3 30.8 %fusion.4 = bf16[376,1024]{1,0:T(8,128)(2,1)S(1)} fusion(bf16[1500,1,1024]{2,0,1:T(8,128)(2,1)} %fusion.79), kind=kCustom, calls=%all-reduce-scatter.4 | all-reduce-scatter fusion | flops 1540097 | bytes 3842560
  959.6 49.6 %all-gather.7.cloned.1.call-done = bf16[1500,1,1024]{2,1,0:T(2,128)(2,1)} async-done(((bf16[375,1,1024]{2,1,0:T(2,128)(2,1)}), bf16[1500,1,1024]{2,1,0:T(2,128)(2,1)}) %all-gather.7.cloned.1.call-update) | async-done | bytes 3072016 | tf_op jit(solution)/shard_map/all_gather | solution.py:80
  1009.2 15.1 multiply_reduce_fusion.12
  1024.3 15.2 multiply_reduce_fusion.16
  1056.2 11.7 pad_add_fusion
  1077.5 30.8 %fusion.5 = bf16[376,1024]{1,0:T(8,128)(2,1)S(1)} fusion(bf16[1500,1,1024]{2,0,1:T(8,128)(2,1)} %fusion.73), kind=kCustom, calls=%all-reduce-scatter.5 | all-reduce-scatter fusion | flops 1540097 | bytes 3842560
  1120.8 49.6 %all-gather.9.cloned.1.call-done = bf16[1500,1,1024]{2,1,0:T(2,128)(2,1)} async-done(((bf16[375,1,1024]{2,1,0:T(2,128)(2,1)}), bf16[1500,1,1024]{2,1,0:T(2,128)(2,1)}) %all-gather.9.cloned.1.call-update) | async-done | bytes 3072016 | tf_op jit(solution)/shard_map/all_gather | solution.py:80
  1177.4 840.8 %while.33 = (s32[]{:T(128)}, bf16[4,1500,64]{1,2,0:T(8,128)(2,1)}, bf16[4,1500,64]{1,2,0:T(8,128)(2,1)}, bf16[4,1500,64]{1,2,0:T(8,128)(2,1)}, f32[4,257]{1,0:T(...) while((s32[]{:T(128)}, bf16[4,1500,64]{1,2,0:T(8,128)(2,1)}, ...), condition=%wide.region_29.30_spmd, body=%wide.region_26.29_spmd.sunk | while | flops 1494280448 | bytes 381868960 | solution.py:247
  1193.3 20.1 tile.37
  1213.4 14.1 slice.676
  1227.5 27.7 reshape.1199
  1322.4 23.1 reshape.1200
  1345.6 11.2 pad_convert_fusion.2
  1356.7 20.2 reshape.1201
  1401.8 20.1 tile.37
  1421.9 14.1 slice.676
  1436.0 27.6 reshape.1199
  1530.8 23.1 reshape.1200
  1553.9 11.2 pad_convert_fusion.2
  1565.1 20.2 reshape.1201
  1610.2 20.1 tile.37
  1630.3 14.1 slice.676
  1644.3 27.6 reshape.1199
  1739.2 23.1 reshape.1200
  1773.5 20.2 reshape.1201
  1818.6 20.1 tile.37
  1838.7 14.1 slice.676
  1852.8 27.6 reshape.1199
  1947.6 23.1 reshape.1200
  1981.9 20.2 reshape.1201
  2025.5 30.8 %fusion.6 = bf16[376,1024]{1,0:T(8,128)(2,1)S(1)} fusion(bf16[1500,1,1024]{2,0,1:T(8,128)(2,1)} %fusion.76), kind=kCustom, calls=%all-reduce-scatter.6 | all-reduce-scatter fusion | flops 1540097 | bytes 3842560
  2162.1 14.5 multiply_reduce_fusion.22
  2187.6 33.7 %fusion.7 = bf16[376,1024]{1,0:T(8,128)(2,1)S(1)} fusion(bf16[1500,1,1024]{2,0,1:T(8,128)(2,1)} %fusion.80), kind=kCustom, calls=%all-reduce-scatter.7 | all-reduce-scatter fusion | flops 1540097 | bytes 3842560
  2224.7 38.8 %all-reduce.85 = (f32[4,257]{1,0:T(4,128)}, f32[31,256]{1,0:T(8,128)}) all-reduce(f32[4,257]{1,0:T(4,128)S(1)} %get-tuple-element.278, f32[31,256]{1,0:T(8,128)S(1)} %pad_add_fusion.7), channel_id=1, replica_groups=mesh['dp'=8,'tensor'=4] {'dp'}, use_global_device_ids=true, to_apply=%region_44.45 | all-reduce | flops 8964 | bytes 71712 | tf_op jit(solution)/shard_map/psum | solution.py:364
  2271.7 38.3 %all-reduce.84 = (f32[1024]{0:T(1024)}, f32[1024]{0:T(1024)}, f32[1024]{0:T(1024)}, f32[1024]{0:T(1024)}, f32[1024]{0:T(1024)}) all-reduce(f32[1024]{0:T(1024)S(1)} %get-tuple-element.454, f32[1024]{0:T(1024)S(1)} %get-tuple-element.446, f32[1024]{0:T(1024)S(1)} %copy-done.112, ...), channel_id=1, replica_groups=mesh['dp'=8,'tensor'=4] {'dp','tensor'}, use_global_device_ids=true, to_apply=%region_37.38 | all-reduce | flops 5120 | bytes 40960 | tf_op jit(solution)/shard_map/psum | solution.py:365
  2311.9 23.5 reduce-scatter.43.cloned.1.call-done
  2335.4 92.2 %reduce-scatter.47.cloned.1.call-done = f32[1024,128]{1,0:T(8,128)} async-done(((f32[1024,1024]{1,0:T(8,128)}), f32[1024,128]{1,0:T(8,128)}) %reduce-scatter.47.cloned.1.call-update) | async-done | bytes 524304 | tf_op jit(solution)/shard_map/reduce_scatter | solution.py:112
  2427.6 92.1 %reduce-scatter.45.cloned.1.call-done = f32[128,1024]{1,0:T(8,128)} async-done(((f32[1024,1024]{1,0:T(8,128)}), f32[128,1024]{1,0:T(8,128)}) %reduce-scatter.45.cloned.1.call-update) | async-done | bytes 524304 | tf_op jit(solution)/shard_map/reduce_scatter | solution.py:111
  2519.6 67.8 %reduce-scatter.39.cloned.1.call-done = f32[256,128]{1,0:T(8,128)} async-done(((f32[256,1024]{1,0:T(8,128)}), f32[256,128]{1,0:T(8,128)}) %reduce-scatter.39.cloned.1.call-update) | async-done | bytes 131088 | tf_op jit(solution)/shard_map/reduce_scatter | solution.py:112
  2587.5 91.7 %reduce-scatter.35.cloned.1.call-done = f32[1024,128]{1,0:T(8,128)} async-done(((f32[1024,1024]{1,0:T(8,128)}), f32[1024,128]{1,0:T(8,128)}) %reduce-scatter.35.cloned.1.call-update) | async-done | bytes 524304 | tf_op jit(solution)/shard_map/reduce_scatter | solution.py:112
  2679.2 92.2 %reduce-scatter.33.cloned.1.call-done = f32[128,1024]{1,0:T(8,128)} async-done(((f32[1024,1024]{1,0:T(8,128)}), f32[128,1024]{1,0:T(8,128)}) %reduce-scatter.33.cloned.1.call-update) | async-done | bytes 524304 | tf_op jit(solution)/shard_map/reduce_scatter | solution.py:111
  (627 shorter events, 975.6 us)
Async XLA Ops:
  7.2 788.7 %copy-start = (bf16[1024,1024]{1,0:T(8,128)(2,1)S(1)}, bf16[1024,1024]{1,0:T(8,128)(2,1)}, u32[]{:S(2)}) copy-start(bf16[1024,1024]{1,0:T(8,128)(2,1)} %param.42) | copy-start | bytes 6291460
  7.2 893.4 %all-gather.5.cloned.1.call-start = ((), (), s32[]{:S(2)}) async-start(), calls=%async_computation.8 | async-start | bytes 7680000 | tf_op jit(solution)/shard_map/all_gather | solution.py:80
  12.0 17.8 collective-permute-start
  12.5 20.3 collective-permute-start.2
  29.8 11.6 collective-permute-start.1
  32.4 113.5 %copy-start.114 = (s32[1024]{0:T(1024)}, s32[1024]{0:T(1024)S(1)}, u32[]{:S(2)}) copy-start(s32[1024]{0:T(1024)S(1)} %pad_clamp_fusion) | copy-start | bytes 12292
  66.6 36.7 %copy-start.128 = (u32[32]{0:T(128)S(1)}, u32[32]{0:T(128)}, u32[]{:S(2)}) copy-start(u32[32]{0:T(128)} %constant.380) | copy-start | bytes 388
  102.0 2.5 collective-permute-start.12
  114.7 15.3 collective-permute-start.3
  117.0 18.3 collective-permute-start.5
  130.1 12.7 collective-permute-start.4
  632.4 2.1 collective-permute-start.13
  643.4 14.5 collective-permute-start.6
  645.9 397.6 %copy-start.81 = (pred[1500]{0:T(1024)(128)(4,1)}, pred[1500]{0:T(1024)(128)(4,1)S(1)}, u32[]{:S(2)}) copy-start(pred[1500]{0:T(1024)(128)(4,1)S(1)} %get-tuple-element.471) | copy-start | bytes 4504
  645.9 397.6 %copy-start.83 = (pred[1500]{0:T(1024)(128)(4,1)}, pred[1500]{0:T(1024)(128)(4,1)S(1)}, u32[]{:S(2)}) copy-start(pred[1500]{0:T(1024)(128)(4,1)S(1)} %get-tuple-element.472) | copy-start | bytes 4504
  645.9 397.6 %copy-start.85 = (pred[1500]{0:T(1024)(128)(4,1)}, pred[1500]{0:T(1024)(128)(4,1)S(1)}, u32[]{:S(2)}) copy-start(pred[1500]{0:T(1024)(128)(4,1)S(1)} %get-tuple-element.473) | copy-start | bytes 4504
  646.0 403.4 %copy-start.75 = (pred[1500]{0:T(1024)(128)(4,1)}, pred[1500]{0:T(1024)(128)(4,1)S(1)}, u32[]{:S(2)}) copy-start(pred[1500]{0:T(1024)(128)(4,1)S(1)} %get-tuple-element.468) | copy-start | bytes 4504
  646.0 403.3 %copy-start.77 = (pred[1500]{0:T(1024)(128)(4,1)}, pred[1500]{0:T(1024)(128)(4,1)S(1)}, u32[]{:S(2)}) copy-start(pred[1500]{0:T(1024)(128)(4,1)S(1)} %get-tuple-element.469) | copy-start | bytes 4504
  646.0 403.3 %copy-start.79 = (pred[1500]{0:T(1024)(128)(4,1)}, pred[1500]{0:T(1024)(128)(4,1)S(1)}, u32[]{:S(2)}) copy-start(pred[1500]{0:T(1024)(128)(4,1)S(1)} %get-tuple-element.470) | copy-start | bytes 4504
  646.2 393.3 %copy-start.95 = (pred[1500]{0:T(1024)(128)(4,1)}, pred[1500]{0:T(1024)(128)(4,1)S(1)}, u32[]{:S(2)}) copy-start(pred[1500]{0:T(1024)(128)(4,1)S(1)} %get-tuple-element.479) | copy-start | bytes 4504
  646.2 393.3 %copy-start.97 = (pred[1500]{0:T(1024)(128)(4,1)}, pred[1500]{0:T(1024)(128)(4,1)S(1)}, u32[]{:S(2)}) copy-start(pred[1500]{0:T(1024)(128)(4,1)S(1)} %get-tuple-element.480) | copy-start | bytes 4504
  646.2 393.3 %copy-start.99 = (pred[1500]{0:T(1024)(128)(4,1)}, pred[1500]{0:T(1024)(128)(4,1)S(1)}, u32[]{:S(2)}) copy-start(pred[1500]{0:T(1024)(128)(4,1)S(1)} %get-tuple-element.481) | copy-start | bytes 4504
  646.3 393.3 %copy-start.101 = (pred[1500]{0:T(1024)(128)(4,1)}, pred[1500]{0:T(1024)(128)(4,1)S(1)}, u32[]{:S(2)}) copy-start(pred[1500]{0:T(1024)(128)(4,1)S(1)} %get-tuple-element.482) | copy-start | bytes 4504
  646.3 397.3 %copy-start.71 = (pred[1500]{0:T(1024)(128)(4,1)}, pred[1500]{0:T(1024)(128)(4,1)S(1)}, u32[]{:S(2)}) copy-start(pred[1500]{0:T(1024)(128)(4,1)S(1)} %get-tuple-element.477) | copy-start | bytes 4504
  646.3 397.3 %copy-start.73 = (pred[1500]{0:T(1024)(128)(4,1)}, pred[1500]{0:T(1024)(128)(4,1)S(1)}, u32[]{:S(2)}) copy-start(pred[1500]{0:T(1024)(128)(4,1)S(1)} %get-tuple-element.478) | copy-start | bytes 4504
  646.3 397.3 %copy-start.87 = (pred[1500]{0:T(1024)(128)(4,1)}, pred[1500]{0:T(1024)(128)(4,1)S(1)}, u32[]{:S(2)}) copy-start(pred[1500]{0:T(1024)(128)(4,1)S(1)} %get-tuple-element.474) | copy-start | bytes 4504
  646.3 397.3 %copy-start.89 = (pred[1500]{0:T(1024)(128)(4,1)}, pred[1500]{0:T(1024)(128)(4,1)S(1)}, u32[]{:S(2)}) copy-start(pred[1500]{0:T(1024)(128)(4,1)S(1)} %get-tuple-element.475) | copy-start | bytes 4504
  646.3 397.3 %copy-start.91 = (pred[1500]{0:T(1024)(128)(4,1)}, pred[1500]{0:T(1024)(128)(4,1)S(1)}, u32[]{:S(2)}) copy-start(pred[1500]{0:T(1024)(128)(4,1)S(1)} %get-tuple-element.476) | copy-start | bytes 4504
  646.6 18.5 collective-permute-start.8
  658.0 13.6 collective-permute-start.7
  664.5 375.1 %copy-start.93 = (pred[1500]{0:T(1024)(128)(4,1)}, pred[1500]{0:T(1024)(128)(4,1)S(1)}, u32[]{:S(2)}) copy-start(pred[1500]{0:T(1024)(128)(4,1)S(1)} %get-tuple-element.483) | copy-start | bytes 4504
  664.5 379.1 %copy-start.65 = (pred[1500]{0:T(1024)(128)(4,1)}, pred[1500]{0:T(1024)(128)(4,1)S(1)}, u32[]{:S(2)}) copy-start(pred[1500]{0:T(1024)(128)(4,1)S(1)} %get-tuple-element.484) | copy-start | bytes 4504
  664.5 384.8 %copy-start.67 = (pred[1500]{0:T(1024)(128)(4,1)}, pred[1500]{0:T(1024)(128)(4,1)S(1)}, u32[]{:S(2)}) copy-start(pred[1500]{0:T(1024)(128)(4,1)S(1)} %get-tuple-element.485) | copy-start | bytes 4504
  738.6 2.1 collective-permute-start.14
  748.6 15.6 collective-permute-start.9
  750.9 18.0 collective-permute-start.11
  764.2 12.6 collective-permute-start.10
  835.0 2.1 collective-permute-start.15
  851.5 157.7 %all-gather.7.cloned.1.call-start = ((), (), s32[]{:S(2)}) async-start(), calls=%async_computation.9 | async-start | bytes 7680000 | tf_op jit(solution)/shard_map/all_gather | solution.py:80
  947.2 2.2 collective-permute-start.16
  957.3 52.0 %copy-start.134 = (bf16[256,1024]{1,0:T(8,128)(2,1)S(1)}, bf16[256,1024]{1,0:T(8,128)(2,1)}, u32[]{:S(2)}) copy-start(bf16[256,1024]{1,0:T(8,128)(2,1)} %param.39) | copy-start | bytes 1572868
  959.6 210.8 %all-gather.9.cloned.1.call-start = ((), (), s32[]{:S(2)}) async-start(), calls=%async_computation.10 | async-start | bytes 7680000 | tf_op jit(solution)/shard_map/all_gather | solution.py:80
  1108.4 2.2 collective-permute-start.17
  1118.4 52.0 %copy-start.135 = (bf16[256,1024]{1,0:T(8,128)(2,1)S(1)}, bf16[256,1024]{1,0:T(8,128)(2,1)}, u32[]{:S(2)}) copy-start(bf16[256,1024]{1,0:T(8,128)(2,1)} %param.34) | copy-start | bytes 1572868
  1120.8 1012.0 %all-gather.11.cloned.1.call-start = ((), (), s32[]{:S(2)}) async-start(), calls=%async_computation.11 | async-start | bytes 7680000 | tf_op jit(solution)/shard_map/all_gather | solution.py:80
  1177.4 840.8 %copy-start.46 = (bf16[1024,256]{1,0:T(8,128)(2,1)S(1)}, bf16[1024,256]{1,0:T(8,128)(2,1)}, u32[]{:S(2)}) copy-start(bf16[1024,256]{1,0:T(8,128)(2,1)} %param.32) | copy-start | bytes 1572868
  2056.4 2.2 collective-permute-start.18
  2069.9 153.0 %reduce-scatter.41.cloned.1.call-start = ((), (), s32[]{:S(2)}) async-start(), calls=%async_computation.16 | async-start | bytes 2359296 | tf_op jit(solution)/shard_map/reduce_scatter | solution.py:111
  2086.2 223.9 %reduce-scatter.37.cloned.1.call-start = ((), (), s32[]{:S(2)}) async-start(), calls=%async_computation.14 | async-start | bytes 3538944 | tf_op jit(solution)/shard_map/reduce_scatter | solution.py:111
  2101.0 234.4 %reduce-scatter.43.cloned.1.call-start = ((), (), s32[]{:S(2)}) async-start(), calls=%async_computation.17 | async-start | bytes 1179648 | tf_op jit(solution)/shard_map/reduce_scatter | solution.py:112
  2107.6 320.0 %reduce-scatter.47.cloned.1.call-start = ((), (), s32[]{:S(2)}) async-start(), calls=%async_computation.19 | async-start | bytes 4718592 | tf_op jit(solution)/shard_map/reduce_scatter | solution.py:112
  2118.3 401.4 %reduce-scatter.45.cloned.1.call-start = ((), (), s32[]{:S(2)}) async-start(), calls=%async_computation.18 | async-start | bytes 4718592 | tf_op jit(solution)/shard_map/reduce_scatter | solution.py:111
  2126.6 460.9 %reduce-scatter.39.cloned.1.call-start = ((), (), s32[]{:S(2)}) async-start(), calls=%async_computation.15 | async-start | bytes 1179648 | tf_op jit(solution)/shard_map/reduce_scatter | solution.py:112
  2132.7 546.5 %reduce-scatter.35.cloned.1.call-start = ((), (), s32[]{:S(2)}) async-start(), calls=%async_computation.13 | async-start | bytes 4718592 | tf_op jit(solution)/shard_map/reduce_scatter | solution.py:112
  2143.1 628.3 %reduce-scatter.33.cloned.1.call-start = ((), (), s32[]{:S(2)}) async-start(), calls=%async_computation.12 | async-start | bytes 4718592 | tf_op jit(solution)/shard_map/reduce_scatter | solution.py:111
  2187.5 35.1 %copy-start.119 = (f32[256]{0:T(256)S(1)}, f32[256]{0:T(256)}, u32[]{:S(2)}) copy-start(f32[256]{0:T(256)} %get-tuple-element.437) | copy-start | bytes 3076
  2187.5 35.1 %copy-start.120 = (f32[256]{0:T(256)S(1)}, f32[256]{0:T(256)}, u32[]{:S(2)}) copy-start(f32[256]{0:T(256)} %get-tuple-element.438) | copy-start | bytes 3076
  2187.5 35.1 %copy-start.121 = (f32[256]{0:T(256)S(1)}, f32[256]{0:T(256)}, u32[]{:S(2)}) copy-start(f32[256]{0:T(256)} %get-tuple-element.439) | copy-start | bytes 3076
  2187.5 35.1 %copy-start.122 = (f32[256]{0:T(256)S(1)}, f32[256]{0:T(256)}, u32[]{:S(2)}) copy-start(f32[256]{0:T(256)} %get-tuple-element.440) | copy-start | bytes 3076
  2187.5 35.1 %copy-start.123 = (f32[256]{0:T(256)S(1)}, f32[256]{0:T(256)}, u32[]{:S(2)}) copy-start(f32[256]{0:T(256)} %get-tuple-element.441) | copy-start | bytes 3076
  2221.2 44.0 %copy-start.54 = (f32[1024]{0:T(1024)S(1)}, f32[1024]{0:T(1024)}, u32[]{:S(2)}) copy-start(f32[1024]{0:T(1024)} %param.27) | copy-start | bytes 12292
  2221.3 44.0 %copy-start.57 = (f32[375]{0:T(512)S(1)}, f32[375]{0:T(512)}, u32[]{:S(2)}) copy-start(f32[375]{0:T(512)} %copy-done.56) | copy-start | bytes 4504
  2221.3 42.3 %collective-permute-start.19 = (bf16[3,1024]{1,0:T(4,128)(2,1)S(1)}, bf16[3,1024]{1,0:T(4,128)(2,1)S(1)}, u32[]{:S(2)}, u32[]{:S(2)}) collective-permute-start(bf16[3,1024]{1,0:T(4,128)(2,1)S(1)} %slice.530), channel_id=1, source_target_pairs={{0,1},{1,2},{2,3},{4,5},{5,6},{6,7},{8,9},{9,10},{10,11},{12,13},{... | collective-permute-start | bytes 18440
  2267.0 504.4 %copy-start.1 = (bf16[1024,1024]{1,0:T(8,128)(2,1)S(1)}, bf16[1024,1024]{1,0:T(8,128)(2,1)}, u32[]{:S(2)}) copy-start(bf16[1024,1024]{1,0:T(8,128)(2,1)} %param.42) | copy-start | bytes 6291460
  (112 other events, 915.4 us)
Sparse Core Ops, SparseCore 0:
  851.6 48.9 all-gather.4
  959.7 49.4 all-gather.6
  1120.9 49.4 all-gather.8
  2070.0 49.4 all-gather.10
  2122.8 67.6 reduce-scatter.40
  2194.0 74.0 reduce-scatter.36
  2272.1 63.3 reduce-scatter.42
  2340.1 87.4 reduce-scatter.46
  2431.8 87.7 reduce-scatter.44
  2523.8 63.5 reduce-scatter.38
  2591.7 87.4 reduce-scatter.34
  2683.7 87.6 reduce-scatter.32
